TPU v7x, 1024 devices: a whole 8x8x8 slice. The times are simulated.
1024 devices in a mesh: context: 64 (over z, x), channel: 16 (over y, core).
Axes of the slice: x: 8, y: 8, z: 8, core: 2. Of those that a mesh axis runs over, the one named last changes fastest.
Arguments:
- first_stream: bfloat16 [16384, 8192], P('context', 'channel'), may hold values from -6 to 6
- value_stream: bfloat16 [16384, 8192], P('context', 'channel'), may hold values from -6 to 6
- short_gate: bfloat16 [16384, 8192], P('context', 'channel'), may hold values from -6 to 6
- out_gate: bfloat16 [16384, 8192], P('context', 'channel'), may hold values from -250 to 250
- mr_filter: float32 [128, 8192], P(None, 'channel'), may hold values from -0.5 to 0.5
- li_residue: float32 [16, 8192], P(None, 'channel'), may hold values from -1.5 to 1.5
- li_rate: float32 [16, 8192], P(None, 'channel'), may hold values from 1.8310548e-05 to 0.05
- li_skip: float32 [8192], P('channel'), may hold values from 0.5 to 1.5
- norm_gain: float32 [8192], P('channel'), may hold values from 0.5 to 1.5
Outputs:
- mixed: bfloat16 [16384, 8192], P('context', 'channel')
All inputs are finite; a program needn't handle non-finite values.
Results may differ from a plain program's by a relative error of at most 0.0064.
Values may be sent and summed in bfloat16 or wider, within the bound.
No kernel may reach another device: no remote copies, remote signals or barrier semaphores. Data moves between devices by JAX's collectives and lax.ppermute only.
A program may use at most 32 MiB of HBM per device.

v0:
```python
import functools

import jax
import jax.numpy as jnp
import numpy as np
from jax import lax
from jax.experimental import pallas as pl
from jax.experimental.pallas import tpu as pltpu
from jax.sharding import PartitionSpec as P

D = 8192
LANES = 128
SUB = 8
INTERPRET = False


def split(value):
    high = value.astype(jnp.bfloat16)
    return high, (value - high.astype(jnp.float32)).astype(jnp.bfloat16)


def dot(left, right):
    return lax.dot_general(left, right, (((1,), (0,)), ((), ())), preferred_element_type=jnp.float32)


def host_split(value):
    high = value.astype(jnp.bfloat16)
    return high, (value - high.astype(np.float64)).astype(jnp.bfloat16)


@functools.cache
def dft_tables(rows, taps):
    total = rows + taps
    bins = np.arange(total // 2)[:, None]
    points = np.arange(total)[None, :]
    angle = np.pi / total * ((2 * bins + 1) * points % (2 * total))
    table = np.concatenate([np.cos(angle), -np.sin(angle)], 0)
    return (
        host_split(table[:, :taps])
        + host_split(table[:, taps:])
        + host_split(table[:, taps:].T * (2.0 / total))
    )


def from_behind(value, axis):
    count = lax.axis_size(axis)
    return lax.ppermute(value, axis, [(source, source + 1) for source in range(count - 1)])


def spectra_kernel(first, value, taps, head_hi, head_lo, body_hi, body_lo, signal_ref, filter_ref):
    product = (first[...].astype(jnp.float32) * value[...].astype(jnp.float32)).astype(jnp.bfloat16)
    signal_ref[...] = dot(body_hi[...], product) + dot(body_lo[...], product)
    tap_hi, tap_lo = split(taps[...])
    filter_ref[...] = (
        dot(head_hi[...], tap_hi) + dot(head_hi[...], tap_lo) + dot(head_lo[...], tap_hi)
    )


def short_kernel(
    signal, response, halo, gate, head_hi, head_lo, back_hi, back_lo, rate,
    mixed_ref, state_ref, prefix_ref, steps_ref,
):
    rows, width = mixed_ref.shape
    modes = rate.shape[0]
    strip = rows // SUB
    half = signal.shape[0] // 2
    before = halo[...]
    spectrum = signal[...] + dot(head_hi[...], before) + dot(head_lo[...], before)
    sig_re, sig_im = spectrum[:half], spectrum[half:]
    fil_re, fil_im = response[:half], response[half:]
    out_hi, out_lo = split(
        jnp.concatenate([sig_re * fil_re - sig_im * fil_im, sig_re * fil_im + sig_im * fil_re], 0)
    )
    short = dot(back_hi[...], out_hi) + dot(back_hi[...], out_lo) + dot(back_lo[...], out_hi)
    mixed = (gate[...].astype(jnp.float32) * short).astype(jnp.bfloat16)
    mixed_ref[...] = mixed
    place = lax.broadcasted_iota(jnp.int32, (SUB, LANES), 0)
    tiles = width // LANES
    for tile in range(tiles):
        lanes = slice(tile * LANES, (tile + 1) * LANES)
        base = tile * rows
        steps_ref[base : base + rows] = mixed[:, lanes].astype(jnp.float32)
        speed = rate[:, lanes]
        decay = jnp.exp(-speed)
        decays = [jnp.broadcast_to(decay[r : r + 1], (SUB, LANES)) for r in range(modes)]
        first = steps_ref[pl.ds(base, SUB, stride=strip)]
        states = [first] * modes
        for step in range(1, strip):
            drive = steps_ref[pl.ds(base + step, SUB, stride=strip)]
            states = [decays[r] * states[r] + drive for r in range(modes)]
        jump = jnp.exp(-strip * speed)
        for r in range(modes):
            leap = jnp.broadcast_to(jump[r : r + 1], (SUB, LANES))
            total = states[r]
            for hop in (1, 2, 4):
                total = total + leap * jnp.where(place >= hop, pltpu.roll(total, hop, 0), 0.0)
                leap = leap * leap
            row = r * tiles + tile
            state_ref[row : row + 1] = total[SUB - 1 :]
            prefix_ref[row * SUB : (row + 1) * SUB] = jnp.where(
                place >= 1, pltpu.roll(total, 1, 0), 0.0
            )


def scan_kernel(state, speed, span, start_ref):
    count = state.shape[0]
    place = lax.broadcasted_iota(jnp.int32, state.shape, 0)
    leap = jnp.exp(-span * speed[...])
    total = jnp.where(place >= 1, pltpu.roll(state[...], 1, 0), 0.0)
    hop = 1
    while hop < count:
        total = total + leap * jnp.where(place >= hop, pltpu.roll(total, hop, 0), 0.0)
        leap = leap * leap
        hop *= 2
    start_ref[...] = total


def long_kernel(
    mixed, start, prefix, rate, residue, skip, gate, gated_ref, power_ref, steps_ref, long_ref
):
    rows, width = mixed.shape
    modes = rate.shape[0]
    strip = rows // SUB
    place = lax.broadcasted_iota(jnp.int32, (SUB, LANES), 0).astype(jnp.float32)
    tiles = width // LANES
    squares = jnp.zeros((rows, LANES), jnp.float32)
    for tile in range(tiles):
        lanes = slice(tile * LANES, (tile + 1) * LANES)
        base = tile * rows
        steps_ref[base : base + rows] = mixed[:, lanes].astype(jnp.float32)
        speed = rate[:, lanes]
        decay = jnp.exp(-speed)
        weight = residue[:, lanes] * jnp.sqrt(2.0 * speed)
        decays = [jnp.broadcast_to(decay[r : r + 1], (SUB, LANES)) for r in range(modes)]
        weights = [jnp.broadcast_to(weight[r : r + 1], (SUB, LANES)) for r in range(modes)]
        states = []
        for r in range(modes):
            row = r * tiles + tile
            fade = jnp.exp(-strip * place * speed[r : r + 1])
            states.append(prefix[row * SUB : (row + 1) * SUB] + fade * start[row : row + 1])
        for step in range(strip):
            drive = steps_ref[pl.ds(base + step, SUB, stride=strip)]
            states = [decays[r] * states[r] + drive for r in range(modes)]
            sums = [weights[r] * states[r] for r in range(modes)]
            while len(sums) > 1:
                sums = [a + b for a, b in zip(sums[::2], sums[1::2])]
            long_ref[pl.ds(step, SUB, stride=strip)] = sums[0]
        out = (long_ref[...] + skip[:, lanes] * steps_ref[base : base + rows]).astype(jnp.bfloat16)
        gated = gate[:, lanes].astype(jnp.float32) * out.astype(jnp.float32)
        gated_ref[:, lanes] = gated
        squares = squares + gated * gated
    power_ref[...] = lax.dot_general(
        jnp.ones((power_ref.shape[0], LANES), jnp.float32),
        squares,
        (((1,), (1,)), ((), ())),
        precision=lax.Precision.HIGHEST,
        preferred_element_type=jnp.float32,
    )


def call(kernel, outs, *args, scratch=()):
    return pl.pallas_call(
        kernel,
        out_shape=[jax.ShapeDtypeStruct(shape, dtype) for shape, dtype in outs],
        scratch_shapes=[pltpu.VMEM(shape, jnp.float32) for shape in scratch],
        interpret=INTERPRET,
    )(*args)


def on_device(
    first_stream,
    value_stream,
    short_gate,
    out_gate,
    mr_filter,
    li_residue,
    li_rate,
    li_skip,
    norm_gain,
):
    rows, width = first_stream.shape
    taps = mr_filter.shape[0]
    modes = li_rate.shape[0]
    tiles = width // LANES
    head_hi, head_lo, body_hi, body_lo, back_hi, back_lo = map(jnp.asarray, dft_tables(rows, taps))
    tail = (
        first_stream[rows - taps :].astype(jnp.float32)
        * value_stream[rows - taps :].astype(jnp.float32)
    ).astype(jnp.bfloat16)
    before = from_behind(tail, "context")
    f32, bf16 = jnp.float32, jnp.bfloat16
    span = rows + taps
    signal, response = call(
        spectra_kernel,
        [((span, width), f32), ((span, width), f32)],
        first_stream, value_stream, mr_filter, head_hi, head_lo, body_hi, body_lo,
    )
    lots = modes * tiles
    speeds = li_rate.reshape(lots, LANES)
    speed = lax.dynamic_slice_in_dim(speeds, lax.axis_index("context"), 1, 0)
    mixed, state, prefix = call(
        short_kernel,
        [((rows, width), bf16), ((lots, LANES), f32), ((lots * SUB, LANES), f32)],
        signal, response, before, short_gate, head_hi, head_lo, back_hi, back_lo, li_rate,
        scratch=[(tiles * rows, LANES)],
    )
    ends = lax.all_to_all(state, "context", split_axis=0, concat_axis=0, tiled=True)
    starts = call(
        lambda s, v, o: scan_kernel(s, v, float(rows), o), [((lots, LANES), f32)], ends, speed
    )[0]
    start = lax.all_to_all(starts, "context", split_axis=0, concat_axis=0, tiled=True)
    peers = lax.axis_size("channel")
    gated, power = call(
        long_kernel,
        [((rows, width), f32), ((peers, rows), f32)],
        mixed, start, prefix, li_rate, li_residue, li_skip[None], out_gate,
        scratch=[(tiles * rows, LANES), (rows, LANES)],
    )
    powers = lax.all_to_all(power, "channel", split_axis=0, concat_axis=0, tiled=True)
    scale = lax.rsqrt(jnp.sum(powers, axis=0) / D + 1e-06)
    return (gated * scale[:, None] * norm_gain[None, :]).astype(jnp.bfloat16)


def solution(mesh):
    assert mesh.shape["context"] * LANES == 16 * 512
    placed = (
        P("context", "channel"),
        P("context", "channel"),
        P("context", "channel"),
        P("context", "channel"),
        P(None, "channel"),
        P(None, "channel"),
        P(None, "channel"),
        P("channel"),
        P("channel"),
    )
    return jax.shard_map(
        on_device, mesh=mesh, in_specs=placed, out_specs=P("context", "channel"), check_vma=False
    )
```

profile of v0, /device:TPU:1, one launch (start us, length us, event | category | flops | bytes accessed | tf_op | source)
XLA Modules:
  0.0 91.6 jit_solution(13780221129816323426)
XLA Ops:
  0.0 0.0 copy-start
  0.0 1.0 %multiply_convert_fusion.1 = bf16[128,512]{1,0:T(8,128)(2,1)S(1)} fusion(bf16[256,512]{1,0:T(8,128)(2,1)} %value.1, bf16[256,512]{1,0:T(8,128)(2,1)} %first.1), kind=kLoop, calls=%fused_computation.1 | loop fusion | flops 262144 | bytes 393216 | tf_op jit(solution)/shard_map/convert_element_type | solution.py:189
  1.0 3.9 %collective-permute-start = (bf16[128,512]{1,0:T(8,128)(2,1)S(1)}, bf16[128,512]{1,0:T(8,128)(2,1)S(1)}, u32[]{:S(2)}, u32[]{:S(2)}) collective-permute-start(bf16[128,512]{1,0:T(8,128)(2,1)S(1)} %multiply_convert_fusion.1), channel_id=1, source_target_pairs={{0,16},{16,32},{32,48},{48,64},{64,80},{80,96},{96,112},{112,128},... | collective-permute-start | bytes 393224 | tf_op jit(solution)/shard_map/ppermute | solution.py:47
  5.0 0.0 copy-done
  5.0 2.9 %shard_map.145 = (f32[384,512]{1,0:T(8,128)}, f32[384,512]{1,0:T(8,128)}) custom-call(bf16[256,512]{1,0:T(8,128)(2,1)} %first.1, bf16[256,512]{1,0:T(8,128)(2,1)} %value.1, f32[128,512]{1,0:T(8,128)} %taps.1, bf16[384,128]{1,0:T(8,128)(2,1)} %constant.29.clone.head_hi, bf16[384,128]{1,0:T(8,128)(2,1)} %constant.30.clone.head_lo, ...), custom_call_target="tpu_custom_call" | custom-call | tf_op jit(solution)/shard_map/pallas_call | solution.py:162
  7.9 0.0 collective-permute-done.halo
  7.9 0.0 copy-start.1
  7.9 0.7 copy-done.1
  8.6 4.4 %shard_map.146 = (bf16[256,512]{1,0:T(8,128)(2,1)}, f32[64,128]{1,0:T(8,128)}, f32[512,128]{1,0:T(8,128)}) custom-call(f32[384,512]{1,0:T(8,128)} %get-tuple-element.12.signal, f32[384,512]{1,0:T(8,128)} %get-tuple-element.13.response, bf16[128,512]{1,0:T(8,128)(2,1)} %copy-done.1, bf16[256,512]{1,0:T(8,128)(2,1)} %gate.2, ...), custom_call_target="tpu_custom_call" | custom-call | tf_op jit(solution)/shard_map/pallas_call | solution.py:162
  13.0 23.7 %all-to-all-start = ((f32[64,1,128]{2,1,0:T(1,128)}), f32[64,1,128]{2,1,0:T(1,128)S(1)}, u32[]{:S(2)}, u32[]{:S(2)}) async-start(f32[64,1,128]{2,1,0:T(1,128)} %bitcast.13), calls=%async_computation | async-start | bytes 65536 | tf_op jit(solution)/shard_map/all_to_all | solution.py:207
  36.7 0.5 constant_dynamic-slice_fusion.v
  37.2 10.3 %all-to-all-done = f32[64,1,128]{2,1,0:T(1,128)S(1)} async-done(((f32[64,1,128]{2,1,0:T(1,128)}), f32[64,1,128]{2,1,0:T(1,128)S(1)}, u32[]{:S(2)}, u32[]{:S(2)}) %all-to-all-start) | async-done | bytes 32800 | tf_op jit(solution)/shard_map/all_to_all | solution.py:207
  47.6 0.0 copy-start.2
  47.6 0.6 copy-done.2
  48.2 1.4 %shard_map.147 = f32[64,128]{1,0:T(8,128)} custom-call(f32[64,128]{1,0:T(8,128)} %bitcast.11, f32[1,128]{1,0:T(1,128)} %constant_dynamic-slice_fusion.v), custom_call_target="tpu_custom_call" | custom-call | tf_op jit(solution)/shard_map/pallas_call | solution.py:162
  49.6 16.0 %all_to_all.31 = f32[64,1,128]{2,1,0:T(1,128)} all-to-all(f32[64,1,128]{2,1,0:T(1,128)} %bitcast.12), channel_id=1, replica_groups=mesh['context'=64,'channel'=16] {'context'}, dimensions={0} | all-to-all | bytes 65536 | tf_op jit(solution)/shard_map/all_to_all | solution.py:211
  65.5 3.7 %shard_map.148 = (f32[256,512]{1,0:T(8,128)}, f32[16,256]{1,0:T(8,128)}) custom-call(bf16[256,512]{1,0:T(8,128)(2,1)} %get-tuple-element.14.mixed, f32[64,128]{1,0:T(8,128)} %bitcast.10, f32[512,128]{1,0:T(8,128)} %get-tuple-element.16.prefix, f32[16,512]{1,0:T(8,128)} %rate.3, f32[16,512]{1,0:T(8,128)} %residue.1, f32[1,512]{1,0:T(1,128)} %bitcast.15, ...), custom_call_target="tpu_custom_call" | custom-call | tf_op jit(solution)/shard_map/pallas_call | solution.py:162
  69.3 0.7 copy.18
  70.0 19.0 %all_to_all.32 = f32[16,1,256]{2,1,0:T(1,128)S(1)} all-to-all(f32[16,1,256]{2,1,0:T(1,128)S(1)} %copy.18), channel_id=1, replica_groups=mesh['context'=64,'channel'=16] {'channel'}, dimensions={0} | all-to-all | bytes 32768 | tf_op jit(solution)/shard_map/all_to_all | solution.py:219
  89.0 0.0 copy-start.3
  89.0 0.7 copy-done.3
  89.7 1.9 %multiply_convert_fusion = bf16[256,512]{1,0:T(8,128)(2,1)} fusion(f32[256,512]{1,0:T(8,128)} %get-tuple-element.17, f32[512]{0:T(512)S(1)} %copy-done.3, f32[256]{0:T(256)S(1)} %add_rsqrt_fusion), kind=kLoop, calls=%fused_computation | loop fusion | flops 393216 | bytes 789504 | tf_op jit(solution)/shard_map/convert_element_type | solution.py:221
  (3 shorter events, 0.0 us)
Async XLA Ops:
  0.0 5.0 %copy-start = (f32[16,512]{1,0:T(8,128)S(1)}, f32[16,512]{1,0:T(8,128)}, u32[]{:S(2)}) copy-start(f32[16,512]{1,0:T(8,128)} %rate.3) | copy-start | bytes 98308
  1.0 6.9 %collective-permute-start = (bf16[128,512]{1,0:T(8,128)(2,1)S(1)}, bf16[128,512]{1,0:T(8,128)(2,1)S(1)}, u32[]{:S(2)}, u32[]{:S(2)}) collective-permute-start(bf16[128,512]{1,0:T(8,128)(2,1)S(1)} %multiply_convert_fusion.1), channel_id=1, source_target_pairs={{0,16},{16,32},{32,48},{48,64},{64,80},{80,96},{96,112},{112,128},... | collective-permute-start | bytes 393224 | tf_op jit(solution)/shard_map/ppermute | solution.py:47
  7.9 0.7 copy-start.1
  13.0 34.6 %all-to-all-start = ((f32[64,1,128]{2,1,0:T(1,128)}), f32[64,1,128]{2,1,0:T(1,128)S(1)}, u32[]{:S(2)}, u32[]{:S(2)}) async-start(f32[64,1,128]{2,1,0:T(1,128)} %bitcast.13), calls=%async_computation | async-start | bytes 65536 | tf_op jit(solution)/shard_map/all_to_all | solution.py:207
  47.6 0.6 copy-start.2
  89.0 0.7 copy-start.3
where the time goes:
time: 92.1 us; the launch traced here: 91.6 us
  blocking collectives  35 us (38%)
  starting transfers between devices  27.6 us (30%)
  Pallas kernels  12.4 us (13%)
  waiting for transfers between devices  10.3 us (11%)
  local copies, waits for them, and re-layouts  3.22 us (3%)
  other arithmetic  2.9 us (3%)
    all_to_all x1, starting transfers between devices, on_device(): lax.all_to_all(state, 'context', split_axis=0, concat_axis=0, tiled=True)  23.7 us
    all_to_all x1, blocking collectives, on_device(): lax.all_to_all(power, 'channel', split_axis=0, concat_axis=0, tiled=True)  19 us
    all_to_all x1, blocking collectives, on_device(): lax.all_to_all(starts, 'context', split_axis=0, concat_axis=0, tiled=True)  16 us
    pallas_call x4, Pallas kernels, call(): pl.pallas_call(kernel, out_shape=[jax.ShapeDtypeStruct(shape, dtype) for...  12.4 us
    all_to_all x1, waiting for transfers between devices, on_device(): lax.all_to_all(state, 'context', split_axis=0, concat_axis=0, tiled=True)  10.3 us
    ppermute x1, starting transfers between devices, from_behind(): lax.ppermute(value, axis, [(source, source + 1) for source in range(count...  3.94 us
    unnamed x8, local copies, waits for them, and re-layouts  1.94 us
    convert_element_type x1, other arithmetic, on_device(): return (gated * scale[:, None] * norm_gain[None, :]).astype(jnp.bfloat16)  1.86 us
  transfers between devices with their start and end apart: 2, of which 1 were waited for; matrix products, arithmetic and copies ran while one was open for 1% of the time, Pallas kernels for 3%

commit v1 on v0

--- a/solution.py
+++ b/solution.py
@@ -1,4 +1,5 @@
 import functools
+import math
 
 import jax
 import jax.numpy as jnp
@@ -45,6 +46,14 @@
 def from_behind(value, axis):
     count = lax.axis_size(axis)
     return lax.ppermute(value, axis, [(source, source + 1) for source in range(count - 1)])
+
+
+def exchange(value, axis, peers, groups):
+    rows, width = value.shape
+    blocks = value.reshape(peers, rows // peers, width)
+    return lax.all_to_all(
+        blocks, axis, split_axis=0, concat_axis=0, tiled=True, axis_index_groups=groups
+    ).reshape(rows, width)
 
 
 def spectra_kernel(first, value, taps, head_hi, head_lo, body_hi, body_lo, signal_ref, filter_ref):
@@ -76,6 +85,7 @@
     mixed_ref[...] = mixed
     place = lax.broadcasted_iota(jnp.int32, (SUB, LANES), 0)
     tiles = width // LANES
+    lots = modes * tiles
     for tile in range(tiles):
         lanes = slice(tile * LANES, (tile + 1) * LANES)
         base = tile * rows
@@ -96,32 +106,42 @@
                 total = total + leap * jnp.where(place >= hop, pltpu.roll(total, hop, 0), 0.0)
                 leap = leap * leap
             row = r * tiles + tile
-            state_ref[row : row + 1] = total[SUB - 1 :]
+            for peer in range(state_ref.shape[0] // lots):
+                state_ref[peer * lots + row : peer * lots + row + 1] = total[SUB - 1 :]
             prefix_ref[row * SUB : (row + 1) * SUB] = jnp.where(
                 place >= 1, pltpu.roll(total, 1, 0), 0.0
             )
 
 
-def scan_kernel(state, speed, span, start_ref):
-    count = state.shape[0]
-    place = lax.broadcasted_iota(jnp.int32, state.shape, 0)
-    leap = jnp.exp(-span * speed[...])
-    total = jnp.where(place >= 1, pltpu.roll(state[...], 1, 0), 0.0)
-    hop = 1
-    while hop < count:
-        total = total + leap * jnp.where(place >= hop, pltpu.roll(total, hop, 0), 0.0)
-        leap = leap * leap
-        hop *= 2
-    start_ref[...] = total
+def chain(parts, position, leap):
+    lots = leap.shape[0]
+    total = parts[:lots]
+    ahead = jnp.zeros_like(total)
+    for part in range(1, parts.shape[0] // lots):
+        ahead = jnp.where(position == part, total, ahead)
+        total = leap * total + parts[part * lots : (part + 1) * lots]
+    return ahead, total
+
+
+def row_kernel(place, states, speeds, ahead_ref, total_ref, *, rows):
+    ahead, total = chain(states, place[0], jnp.exp(-rows * speeds[...]))
+    ahead_ref[...] = ahead
+    lots = ahead.shape[0]
+    for peer in range(total_ref.shape[0] // lots):
+        total_ref[peer * lots : (peer + 1) * lots] = total
 
 
 def long_kernel(
-    mixed, start, prefix, rate, residue, skip, gate, gated_ref, power_ref, steps_ref, long_ref
+    place, mixed, totals, ahead, speeds, prefix, rate, residue, skip, gate,
+    gated_ref, power_ref, steps_ref, long_ref,
 ):
     rows, width = mixed.shape
+    side = totals.shape[0] // speeds.shape[0]
+    above, _ = chain(totals, place[1], jnp.exp(-float(side * rows) * speeds[...]))
+    start = ahead[...] + jnp.exp(-(place[0] * rows).astype(jnp.float32) * speeds[...]) * above
     modes = rate.shape[0]
     strip = rows // SUB
-    place = lax.broadcasted_iota(jnp.int32, (SUB, LANES), 0).astype(jnp.float32)
+    order = lax.broadcasted_iota(jnp.int32, (SUB, LANES), 0)
     tiles = width // LANES
     squares = jnp.zeros((rows, LANES), jnp.float32)
     for tile in range(tiles):
@@ -136,7 +156,7 @@
         states = []
         for r in range(modes):
             row = r * tiles + tile
-            fade = jnp.exp(-strip * place * speed[r : r + 1])
+            fade = jnp.exp(-(strip * order).astype(jnp.float32) * speed[r : r + 1])
             states.append(prefix[row * SUB : (row + 1) * SUB] + fade * start[row : row + 1])
         for step in range(strip):
             drive = steps_ref[pl.ds(base + step, SUB, stride=strip)]
@@ -149,22 +169,47 @@
         gated = gate[:, lanes].astype(jnp.float32) * out.astype(jnp.float32)
         gated_ref[:, lanes] = gated
         squares = squares + gated * gated
-    power_ref[...] = lax.dot_general(
-        jnp.ones((power_ref.shape[0], LANES), jnp.float32),
+    sums = lax.dot_general(
+        jnp.ones((SUB, LANES), jnp.float32),
         squares,
         (((1,), (1,)), ((), ())),
         precision=lax.Precision.HIGHEST,
         preferred_element_type=jnp.float32,
     )
-
-
-def call(kernel, outs, *args, scratch=()):
+    packed = jnp.zeros((SUB, LANES), jnp.float32)
+    for block in range(rows // LANES):
+        packed = jnp.where(order == block, sums[:, block * LANES : (block + 1) * LANES], packed)
+    for peer in range(power_ref.shape[0] // SUB):
+        power_ref[peer * SUB : (peer + 1) * SUB] = packed
+
+
+def norm_kernel(powers, gated, gain, out_ref, *, channels):
+    rows = gated.shape[0]
+    total = powers[:SUB]
+    for peer in range(1, powers.shape[0] // SUB):
+        total = total + powers[peer * SUB : (peer + 1) * SUB]
+    scale = lax.rsqrt(total / channels + 1e-06)
+    for block in range(rows // LANES):
+        column = jnp.broadcast_to(scale[block : block + 1], (LANES, LANES)).T
+        tokens = slice(block * LANES, (block + 1) * LANES)
+        for tile in range(gated.shape[1] // LANES):
+            lanes = slice(tile * LANES, (tile + 1) * LANES)
+            out_ref[tokens, lanes] = (gated[tokens, lanes] * column * gain[:, lanes]).astype(
+                jnp.bfloat16
+            )
+
+
+def call(kernel, outs, *args, scratch=(), place=None):
+    vmem = pl.BlockSpec(memory_space=pltpu.VMEM)
+    lead = () if place is None else (place,)
     return pl.pallas_call(
         kernel,
         out_shape=[jax.ShapeDtypeStruct(shape, dtype) for shape, dtype in outs],
+        in_specs=[pl.BlockSpec(memory_space=pltpu.SMEM)] * len(lead) + [vmem] * len(args),
+        out_specs=[vmem] * len(outs),
         scratch_shapes=[pltpu.VMEM(shape, jnp.float32) for shape in scratch],
         interpret=INTERPRET,
-    )(*args)
+    )(*lead, *args)
 
 
 def on_device(
@@ -197,32 +242,41 @@
     )
     lots = modes * tiles
     speeds = li_rate.reshape(lots, LANES)
-    speed = lax.dynamic_slice_in_dim(speeds, lax.axis_index("context"), 1, 0)
-    mixed, state, prefix = call(
+    shards = lax.axis_size("context")
+    side = math.isqrt(shards)
+    along_x = [[z * side + x for x in range(side)] for z in range(side)]
+    along_z = [[z * side + x for z in range(side)] for x in range(side)]
+    shard = lax.axis_index("context")
+    place = jnp.stack([shard % side, shard // side])
+    mixed, states, prefix = call(
         short_kernel,
-        [((rows, width), bf16), ((lots, LANES), f32), ((lots * SUB, LANES), f32)],
+        [((rows, width), bf16), ((side * lots, LANES), f32), ((lots * SUB, LANES), f32)],
         signal, response, before, short_gate, head_hi, head_lo, back_hi, back_lo, li_rate,
         scratch=[(tiles * rows, LANES)],
     )
-    ends = lax.all_to_all(state, "context", split_axis=0, concat_axis=0, tiled=True)
-    starts = call(
-        lambda s, v, o: scan_kernel(s, v, float(rows), o), [((lots, LANES), f32)], ends, speed
-    )[0]
-    start = lax.all_to_all(starts, "context", split_axis=0, concat_axis=0, tiled=True)
+    states = exchange(states, "context", side, along_x)
+    ahead, totals = call(
+        functools.partial(row_kernel, rows=float(rows)),
+        [((lots, LANES), f32), ((side * lots, LANES), f32)],
+        states, speeds, place=place,
+    )
+    totals = exchange(totals, "context", side, along_z)
     peers = lax.axis_size("channel")
     gated, power = call(
         long_kernel,
-        [((rows, width), f32), ((peers, rows), f32)],
-        mixed, start, prefix, li_rate, li_residue, li_skip[None], out_gate,
-        scratch=[(tiles * rows, LANES), (rows, LANES)],
-    )
-    powers = lax.all_to_all(power, "channel", split_axis=0, concat_axis=0, tiled=True)
-    scale = lax.rsqrt(jnp.sum(powers, axis=0) / D + 1e-06)
-    return (gated * scale[:, None] * norm_gain[None, :]).astype(jnp.bfloat16)
+        [((rows, width), f32), ((peers * SUB, LANES), f32)],
+        mixed, totals, ahead, speeds, prefix, li_rate, li_residue, li_skip[None], out_gate,
+        scratch=[(tiles * rows, LANES), (rows, LANES)], place=place,
+    )
+    powers = exchange(power, "channel", peers, None)
+    return call(
+        functools.partial(norm_kernel, channels=float(D)),
+        [((rows, width), bf16)],
+        powers, gated, norm_gain[None],
+    )[0]
 
 
 def solution(mesh):
-    assert mesh.shape["context"] * LANES == 16 * 512
     placed = (
         P("context", "channel"),
         P("context", "channel"),

time: 92.1 us -> 85.5 us (0.928)
  starting transfers between devices: 27.6 us -> 12.1 us
  blocking collectives: 35 us -> 46.1 us
  Pallas kernels: 12.4 us -> 15 us
  waiting for transfers between devices: 10.3 us -> 8.11 us
  other arithmetic: 2.9 us -> 1.61 us
  local copies, waits for them, and re-layouts: 3.22 us -> 1.97 us
    all_to_all x1, starting transfers between devices: 23.7 us -> 8.15 us  [exchange(): lax.all_to_all(blocks, axis, split_axis=0, concat_axis=0, tiled=True, axi...]
    all_to_all x2, blocking collectives: 35 us -> 46.1 us  [exchange(): lax.all_to_all(blocks, axis, split_axis=0, concat_axis=0, tiled=True, axi...]
    pallas_call x4 -> x5, Pallas kernels: 12.4 us -> 15 us  [call(): pl.pallas_call(kernel, out_shape=[jax.ShapeDtypeStruct(shape, dtype) for...]
    all_to_all x1, waiting for transfers between devices: 10.3 us -> 8.11 us  [exchange(): lax.all_to_all(blocks, axis, split_axis=0, concat_axis=0, tiled=True, axi...]
    convert_element_type x1 -> x0, other arithmetic: 1.86 us -> none  [on_device(): return (gated * scale[:, None] * norm_gain[None, :]).astype(jnp.bfloat16)]
    unnamed x8 -> x6, local copies, waits for them, and re-layouts: 1.94 us -> 1.36 us
where the time goes in v1:
time: 85.5 us; the launch traced here: 84.9 us
  blocking collectives  46.1 us (54%)
  Pallas kernels  15 us (18%)
  starting transfers between devices  12.1 us (14%)
  waiting for transfers between devices  8.11 us (9%)
  local copies, waits for them, and re-layouts  1.97 us (2%)
  other arithmetic  1.61 us (2%)
    all_to_all x2, blocking collectives, exchange(): lax.all_to_all(blocks, axis, split_axis=0, concat_axis=0, tiled=True, axi...  46.1 us
    pallas_call x5, Pallas kernels, call(): pl.pallas_call(kernel, out_shape=[jax.ShapeDtypeStruct(shape, dtype) for...  15 us
    all_to_all x1, starting transfers between devices, exchange(): lax.all_to_all(blocks, axis, split_axis=0, concat_axis=0, tiled=True, axi...  8.15 us
    all_to_all x1, waiting for transfers between devices, exchange(): lax.all_to_all(blocks, axis, split_axis=0, concat_axis=0, tiled=True, axi...  8.11 us
    ppermute x1, starting transfers between devices, from_behind(): lax.ppermute(value, axis, [(source, source + 1) for source in range(count...  3.94 us
  transfers between devices with their start and end apart: 2, of which 1 were waited for; matrix products, arithmetic and copies ran while one was open for 1% of the time, Pallas kernels for 3%

profile of v1, /device:TPU:1, one launch (start us, length us, event | category | flops | bytes accessed | tf_op | source)
XLA Modules:
  0.0 84.9 jit_solution(1064331960241443276)
XLA Ops:
  0.0 1.0 %multiply_convert_fusion = bf16[128,512]{1,0:T(8,128)(2,1)S(1)} fusion(bf16[256,512]{1,0:T(8,128)(2,1)} %value.1, bf16[256,512]{1,0:T(8,128)(2,1)} %first.1), kind=kLoop, calls=%fused_computation | loop fusion | flops 262144 | bytes 393216 | tf_op jit(solution)/shard_map/convert_element_type | solution.py:234
  1.0 3.9 %collective-permute-start = (bf16[128,512]{1,0:T(8,128)(2,1)S(1)}, bf16[128,512]{1,0:T(8,128)(2,1)S(1)}, u32[]{:S(2)}, u32[]{:S(2)}) collective-permute-start(bf16[128,512]{1,0:T(8,128)(2,1)S(1)} %multiply_convert_fusion), channel_id=1, source_target_pairs={{0,16},{16,32},{32,48},{48,64},{64,80},{80,96},{96,112},{112,128},... | collective-permute-start | bytes 393224 | tf_op jit(solution)/shard_map/ppermute | solution.py:48
  5.0 3.0 %shard_map.145 = (f32[384,512]{1,0:T(8,128)}, f32[384,512]{1,0:T(8,128)}) custom-call(bf16[256,512]{1,0:T(8,128)(2,1)} %first.1, bf16[256,512]{1,0:T(8,128)(2,1)} %value.1, f32[128,512]{1,0:T(8,128)} %taps.1, bf16[384,128]{1,0:T(8,128)(2,1)} %constant.44.clone.head_hi, bf16[384,128]{1,0:T(8,128)(2,1)} %constant.45.clone.head_lo, ...), custom_call_target="tpu_custom_call" | custom-call | tf_op jit(solution)/shard_map/pallas_call | solution.py:205
  7.9 0.0 collective-permute-done.halo
  7.9 0.0 copy-start.2
  7.9 0.7 copy-done.2
  8.6 4.5 %shard_map.146 = (bf16[256,512]{1,0:T(8,128)(2,1)}, f32[512,128]{1,0:T(8,128)}, f32[512,128]{1,0:T(8,128)}) custom-call(f32[384,512]{1,0:T(8,128)} %get-tuple-element.14.signal, f32[384,512]{1,0:T(8,128)} %get-tuple-element.15.response, bf16[128,512]{1,0:T(8,128)(2,1)} %copy-done.2, bf16[256,512]{1,0:T(8,128)(2,1)} %gate.2, ...), custom_call_target="tpu_custom_call" | custom-call | tf_op jit(solution)/shard_map/pallas_call | solution.py:205
  13.1 0.0 copy-start.1
  13.1 8.1 %all-to-all-start = ((f32[8,64,128]{2,1,0:T(8,128)}), f32[8,64,128]{2,1,0:T(8,128)S(1)}, u32[]{:S(2)}, u32[]{:S(2)}) async-start(f32[8,64,128]{2,1,0:T(8,128)} %bitcast.12), calls=%async_computation | async-start | bytes 524288 | tf_op jit(solution)/shard_map/all_to_all | solution.py:54
  21.2 0.0 copy-done.1
  21.2 0.6 reshape.23.speeds
  21.8 0.6 pad_add_fusion.place
  22.5 8.1 %all-to-all-done = f32[8,64,128]{2,1,0:T(8,128)S(1)} async-done(((f32[8,64,128]{2,1,0:T(8,128)}), f32[8,64,128]{2,1,0:T(8,128)S(1)}, u32[]{:S(2)}, u32[]{:S(2)}) %all-to-all-start) | async-done | bytes 262176 | tf_op jit(solution)/shard_map/all_to_all | solution.py:54
  30.6 0.0 copy-start
  30.6 0.7 copy-done
  31.3 1.7 %shard_map.147 = (f32[64,128]{1,0:T(8,128)}, f32[512,128]{1,0:T(8,128)}) custom-call(s32[2]{0:T(128)} %pad_add_fusion.place, f32[512,128]{1,0:T(8,128)} %bitcast.10, f32[64,128]{1,0:T(8,128)} %reshape.23.speeds), custom_call_target="tpu_custom_call" | custom-call | tf_op jit(solution)/shard_map/pallas_call | solution.py:205
  33.0 26.1 %all_to_all.15 = f32[8,64,128]{2,1,0:T(8,128)} all-to-all(f32[8,64,128]{2,1,0:T(8,128)} %bitcast.13), channel_id=1, replica_groups={{0,128,256,384,512,640,768,896},{16,144,272,400,528,656,784,912},{32,16..., dimensions={0} | all-to-all | bytes 524288 | tf_op jit(solution)/shard_map/all_to_all | solution.py:54
  59.1 3.9 %shard_map.148 = (f32[256,512]{1,0:T(8,128)}, f32[128,128]{1,0:T(8,128)}) custom-call(s32[2]{0:T(128)} %pad_add_fusion.place, bf16[256,512]{1,0:T(8,128)(2,1)} %get-tuple-element.16.mixed, f32[512,128]{1,0:T(8,128)} %bitcast.11, f32[64,128]{1,0:T(8,128)} %get-tuple-element.19.ahead, f32[64,128]{1,0:T(8,128)} %reshape.23.speeds, ...), custom_call_target="tpu_custom_call" | custom-call | tf_op jit(solution)/shard_map/pallas_call | solution.py:205
  63.0 20.0 %all_to_all.16 = f32[16,8,128]{2,1,0:T(8,128)} all-to-all(f32[16,8,128]{2,1,0:T(8,128)} %bitcast.15), channel_id=1, replica_groups=mesh['context'=64,'channel'=16] {'channel'}, dimensions={0} | all-to-all | bytes 131072 | tf_op jit(solution)/shard_map/all_to_all | solution.py:54
  83.0 1.9 %shard_map.149 = bf16[256,512]{1,0:T(8,128)(2,1)} custom-call(f32[128,128]{1,0:T(8,128)} %bitcast.14, f32[256,512]{1,0:T(8,128)} %get-tuple-element.22.gated, f32[1,512]{1,0:T(1,128)} %bitcast.17), custom_call_target="tpu_custom_call" | custom-call | tf_op jit(solution)/shard_map/pallas_call | solution.py:205
Async XLA Ops:
  1.0 6.9 %collective-permute-start = (bf16[128,512]{1,0:T(8,128)(2,1)S(1)}, bf16[128,512]{1,0:T(8,128)(2,1)S(1)}, u32[]{:S(2)}, u32[]{:S(2)}) collective-permute-start(bf16[128,512]{1,0:T(8,128)(2,1)S(1)} %multiply_convert_fusion), channel_id=1, source_target_pairs={{0,16},{16,32},{32,48},{48,64},{64,80},{80,96},{96,112},{112,128},... | collective-permute-start | bytes 393224 | tf_op jit(solution)/shard_map/ppermute | solution.py:48
  7.9 0.7 copy-start.2
  13.1 8.2 %copy-start.1 = (f32[16,512]{1,0:T(8,128)S(1)}, f32[16,512]{1,0:T(8,128)}, u32[]{:S(2)}) copy-start(f32[16,512]{1,0:T(8,128)} %rate.3) | copy-start | bytes 98308
  13.1 17.5 %all-to-all-start = ((f32[8,64,128]{2,1,0:T(8,128)}), f32[8,64,128]{2,1,0:T(8,128)S(1)}, u32[]{:S(2)}, u32[]{:S(2)}) async-start(f32[8,64,128]{2,1,0:T(8,128)} %bitcast.12), calls=%async_computation | async-start | bytes 524288 | tf_op jit(solution)/shard_map/all_to_all | solution.py:54
  30.6 0.7 copy-start

commit v2 on v1

v2 whole, which is shorter than its diff:
```python
import functools
import math

import jax
import jax.numpy as jnp
import numpy as np
from jax import lax
from jax.experimental import pallas as pl
from jax.experimental.pallas import tpu as pltpu
from jax.sharding import PartitionSpec as P

D = 8192
LANES = 128
SUB = 8
INTERPRET = False


def split(value):
    high = value.astype(jnp.bfloat16)
    return high, (value - high.astype(jnp.float32)).astype(jnp.bfloat16)


def dot(left, right):
    return lax.dot_general(left, right, (((1,), (0,)), ((), ())), preferred_element_type=jnp.float32)


def host_split(value):
    high = value.astype(jnp.bfloat16)
    return high, (value - high.astype(np.float64)).astype(jnp.bfloat16)


@functools.cache
def dft_tables(rows, taps):
    total = rows + taps
    bins = np.arange(total // 2)[:, None]
    points = np.arange(total)[None, :]
    angle = np.pi / total * ((2 * bins + 1) * points % (2 * total))
    table = np.concatenate([np.cos(angle), -np.sin(angle)], 0)
    return (
        host_split(table[:, :taps])
        + host_split(table[:, taps:])
        + host_split(table[:, taps:].T * (2.0 / total))
    )


def from_behind(value, axis):
    count = lax.axis_size(axis)
    return lax.ppermute(value, axis, [(source, source + 1) for source in range(count - 1)])


def exchange(value, axis, peers, groups):
    rows, width = value.shape
    blocks = value.reshape(peers, rows // peers, width)
    return lax.all_to_all(
        blocks, axis, split_axis=0, concat_axis=0, tiled=True, axis_index_groups=groups
    ).reshape(rows, width)


def end_states(mixed, rate, prefix_ref, end_ref, steps_ref):
    rows, width = mixed.shape
    modes = rate.shape[0]
    strip = rows // SUB
    order = lax.broadcasted_iota(jnp.int32, (SUB, LANES), 0)
    for tile in range(width // LANES):
        lanes = slice(tile * LANES, (tile + 1) * LANES)
        base = tile * rows
        steps_ref[base : base + rows] = mixed[:, lanes].astype(jnp.float32)
        speed = rate[:, lanes]
        decay = jnp.exp(-speed)
        decays = [jnp.broadcast_to(decay[r : r + 1], (SUB, LANES)) for r in range(modes)]
        states = [steps_ref[pl.ds(base, SUB, stride=strip)]] * modes
        for step in range(1, strip):
            drive = steps_ref[pl.ds(base + step, SUB, stride=strip)]
            states = [decays[r] * states[r] + drive for r in range(modes)]
        jump = jnp.exp(-strip * speed)
        for r in range(modes):
            leap = jnp.broadcast_to(jump[r : r + 1], (SUB, LANES))
            total = states[r]
            for hop in (1, 2, 4):
                total = total + leap * jnp.where(order >= hop, pltpu.roll(total, hop, 0), 0.0)
                leap = leap * leap
            row = tile * modes + r
            end_ref[row : row + 1] = total[SUB - 1 :]
            prefix_ref[row * SUB : (row + 1) * SUB] = jnp.where(
                order >= 1, pltpu.roll(total, 1, 0), 0.0
            )


def respond(spectrum, response, back_hi, back_lo):
    half = spectrum.shape[0] // 2
    sig_re, sig_im = spectrum[:half], spectrum[half:]
    fil_re, fil_im = response[:half], response[half:]
    out_hi, out_lo = split(
        jnp.concatenate([sig_re * fil_re - sig_im * fil_im, sig_re * fil_im + sig_im * fil_re], 0)
    )
    return dot(back_hi, out_hi) + dot(back_hi, out_lo) + dot(back_lo, out_hi)


def local_kernel(
    first, value, taps, gate, head_hi, head_lo, body_hi, body_lo, back_hi, back_lo, rate, skip, gain,
    response_ref, short_ref, mixed_ref, prefix_ref, end_ref, rows_ref, steps_ref,
):
    rows_ref[0:1] = skip[...]
    rows_ref[1:2] = gain[...]
    product = (first[...].astype(jnp.float32) * value[...].astype(jnp.float32)).astype(jnp.bfloat16)
    spectrum = dot(body_hi[...], product) + dot(body_lo[...], product)
    tap_hi, tap_lo = split(taps[...])
    response = dot(head_hi[...], tap_hi) + dot(head_hi[...], tap_lo) + dot(head_lo[...], tap_hi)
    response_ref[...] = response
    short = respond(spectrum, response, back_hi[...], back_lo[...])
    half = mixed_ref.shape[0]
    short_ref[...] = short[:half]
    mixed = (gate[half:].astype(jnp.float32) * short[half:]).astype(jnp.bfloat16)
    mixed_ref[...] = mixed
    end_states(mixed, rate, prefix_ref, end_ref, steps_ref)


def halo_kernel(
    response, short, halo, gate, head_hi, head_lo, back_hi, back_lo, rate, last,
    mixed_ref, prefix_ref, end_ref, state_ref, steps_ref,
):
    half = mixed_ref.shape[0]
    before = halo[...]
    spectrum = dot(head_hi[...], before) + dot(head_lo[...], before)
    whole = short[...] + respond(spectrum, response, back_hi[:half], back_lo[:half])
    mixed = (gate[:half].astype(jnp.float32) * whole).astype(jnp.bfloat16)
    mixed_ref[...] = mixed
    end_states(mixed, rate, prefix_ref, end_ref, steps_ref)
    state = jnp.exp(-float(half) * stacked(rate)) * end_ref[...] + last[...]
    lots = state.shape[0]
    for peer in range(state_ref.shape[0] // lots):
        state_ref[peer * lots : (peer + 1) * lots] = state


def stacked(rate):
    value = rate[...]
    return jnp.concatenate(
        [value[:, lane : lane + LANES] for lane in range(0, value.shape[1], LANES)], 0
    )


def chain(parts, position, leap):
    lots = leap.shape[0]
    total = parts[:lots]
    ahead = jnp.zeros_like(total)
    for part in range(1, parts.shape[0] // lots):
        ahead = jnp.where(position == part, total, ahead)
        total = leap * total + parts[part * lots : (part + 1) * lots]
    return ahead, total


def row_kernel(states, rate, ahead_ref, total_ref, *, rows, side):
    position = lax.rem(lax.axis_index("context"), side)
    ahead, total = chain(states, position, jnp.exp(-float(rows) * stacked(rate)))
    ahead_ref[...] = ahead
    lots = ahead.shape[0]
    for peer in range(total_ref.shape[0] // lots):
        total_ref[peer * lots : (peer + 1) * lots] = total


def long_kernel(
    mixed_head, mixed_tail, prefix_head, prefix_tail, end, totals, ahead, rate, residue, per_channel, gate,
    gated_ref, power_ref, steps_ref, long_ref, *, side,
):
    half, width = mixed_head.shape
    rows = 2 * half
    modes = rate.shape[0]
    strip = half // SUB
    shard = lax.axis_index("context")
    speeds = stacked(rate)
    above, _ = chain(totals, lax.div(shard, side), jnp.exp(-float(side * rows) * speeds))
    shift = (lax.rem(shard, side) * rows).astype(jnp.float32)
    start = ahead[...] + jnp.exp(-shift * speeds) * above
    middle = jnp.exp(-float(half) * speeds) * start + end[...]
    order = lax.broadcasted_iota(jnp.int32, (SUB, LANES), 0)
    offset = (strip * order).astype(jnp.float32)
    squares = [jnp.zeros((half, LANES), jnp.float32) for _ in range(2)]
    for tile in range(width // LANES):
        lanes = slice(tile * LANES, (tile + 1) * LANES)
        speed = rate[:, lanes]
        decay = jnp.exp(-speed)
        weight = residue[:, lanes] * jnp.sqrt(2.0 * speed)
        decays = [jnp.broadcast_to(decay[r : r + 1], (SUB, LANES)) for r in range(modes)]
        weights = [jnp.broadcast_to(weight[r : r + 1], (SUB, LANES)) for r in range(modes)]
        fades = [jnp.exp(-offset * speed[r : r + 1]) for r in range(modes)]
        for part, (mixed, prefix, begin) in enumerate(
            ((mixed_head, prefix_head, start), (mixed_tail, prefix_tail, middle))
        ):
            base = (2 * tile + part) * half
            steps_ref[base : base + half] = mixed[:, lanes].astype(jnp.float32)
            states = []
            for r in range(modes):
                row = tile * modes + r
                states.append(
                    prefix[row * SUB : (row + 1) * SUB] + fades[r] * begin[row : row + 1]
                )
            for step in range(strip):
                drive = steps_ref[pl.ds(base + step, SUB, stride=strip)]
                states = [decays[r] * states[r] + drive for r in range(modes)]
                sums = [weights[r] * states[r] for r in range(modes)]
                while len(sums) > 1:
                    sums = [a + b for a, b in zip(sums[::2], sums[1::2])]
                long_ref[pl.ds(base + step, SUB, stride=strip)] = sums[0]
            out = (
                long_ref[base : base + half] + per_channel[0:1, lanes] * steps_ref[base : base + half]
            ).astype(jnp.bfloat16)
            tokens = slice(part * half, (part + 1) * half)
            gated = gate[tokens, lanes].astype(jnp.float32) * out.astype(jnp.float32)
            gated_ref[tokens, lanes] = gated * per_channel[1:2, lanes]
            squares[part] = squares[part] + gated * gated
    packed = jnp.zeros((SUB, LANES), jnp.float32)
    for part in range(2):
        sums = lax.dot_general(
            jnp.ones((SUB, LANES), jnp.float32),
            squares[part],
            (((1,), (1,)), ((), ())),
            precision=lax.Precision.HIGHEST,
            preferred_element_type=jnp.float32,
        )
        packed = jnp.where(order == part, sums, packed)
    for peer in range(power_ref.shape[0] // SUB):
        power_ref[peer * SUB : (peer + 1) * SUB] = packed


def norm_kernel(powers, gated, out_ref, *, channels):
    rows = gated.shape[0]
    total = powers[:SUB]
    for peer in range(1, powers.shape[0] // SUB):
        total = total + powers[peer * SUB : (peer + 1) * SUB]
    scale = lax.rsqrt(total / channels + 1e-06)
    for block in range(rows // LANES):
        column = jnp.broadcast_to(scale[block : block + 1], (LANES, LANES)).T
        tokens = slice(block * LANES, (block + 1) * LANES)
        for tile in range(gated.shape[1] // LANES):
            lanes = slice(tile * LANES, (tile + 1) * LANES)
            out_ref[tokens, lanes] = (gated[tokens, lanes] * column).astype(jnp.bfloat16)


def call(kernel, outs, *args, scratch=()):
    vmem = pl.BlockSpec(memory_space=pltpu.VMEM)
    return pl.pallas_call(
        kernel,
        out_shape=[jax.ShapeDtypeStruct(shape, dtype) for shape, dtype in outs],
        in_specs=[vmem] * len(args),
        out_specs=[vmem] * len(outs),
        scratch_shapes=[pltpu.VMEM(shape, jnp.float32) for shape in scratch],
        compiler_params=pltpu.CompilerParams(vmem_limit_bytes=16 << 20),
        interpret=INTERPRET,
    )(*args)


def on_device(
    first_stream,
    value_stream,
    short_gate,
    out_gate,
    mr_filter,
    li_residue,
    li_rate,
    li_skip,
    norm_gain,
):
    rows, width = first_stream.shape
    taps = mr_filter.shape[0]
    modes = li_rate.shape[0]
    tiles = width // LANES
    head_hi, head_lo, body_hi, body_lo, back_hi, back_lo = map(jnp.asarray, dft_tables(rows, taps))
    tail = (
        first_stream[rows - taps :].astype(jnp.float32)
        * value_stream[rows - taps :].astype(jnp.float32)
    ).astype(jnp.bfloat16)
    before = from_behind(tail, "context")
    f32, bf16 = jnp.float32, jnp.bfloat16
    half = rows // 2
    assert half == taps == LANES
    lots = modes * tiles
    strips = (lots * SUB, LANES)
    response, short, mixed_tail, prefix_tail, last, per_channel = call(
        local_kernel,
        [
            ((rows + taps, width), f32), ((half, width), f32), ((half, width), bf16),
            (strips, f32), ((lots, LANES), f32), ((2, width), f32),
        ],
        first_stream, value_stream, mr_filter, short_gate,
        head_hi, head_lo, body_hi, body_lo, back_hi, back_lo, li_rate, li_skip[None], norm_gain[None],
        scratch=[(tiles * half, LANES)],
    )
    side = math.isqrt(lax.axis_size("context"))
    along_x = [[z * side + x for x in range(side)] for z in range(side)]
    along_z = [[z * side + x for z in range(side)] for x in range(side)]
    mixed_head, prefix_head, end, states = call(
        halo_kernel,
        [
            ((half, width), bf16), (strips, f32), ((lots, LANES), f32),
            ((side * lots, LANES), f32),
        ],
        response, short, before, short_gate, head_hi, head_lo, back_hi, back_lo, li_rate, last,
        scratch=[(tiles * half, LANES)],
    )
    states = exchange(states, "context", side, along_x)
    ahead, totals = call(
        functools.partial(row_kernel, rows=rows, side=side),
        [((lots, LANES), f32), ((side * lots, LANES), f32)],
        states, li_rate,
    )
    totals = exchange(totals, "context", side, along_z)
    peers = lax.axis_size("channel")
    gated, power = call(
        functools.partial(long_kernel, side=side),
        [((rows, width), f32), ((peers * SUB, LANES), f32)],
        mixed_head, mixed_tail, prefix_head, prefix_tail, end, totals, ahead,
        li_rate, li_residue, per_channel, out_gate,
        scratch=[(tiles * rows, LANES), (tiles * rows, LANES)],
    )
    powers = exchange(power, "channel", peers, None)
    return call(
        functools.partial(norm_kernel, channels=float(D)),
        [((rows, width), bf16)],
        powers, gated,
    )[0]


def solution(mesh):
    placed = (
        P("context", "channel"),
        P("context", "channel"),
        P("context", "channel"),
        P("context", "channel"),
        P(None, "channel"),
        P(None, "channel"),
        P(None, "channel"),
        P("channel"),
        P("channel"),
    )
    return jax.shard_map(
        on_device, mesh=mesh, in_specs=placed, out_specs=P("context", "channel"), check_vma=False
    )
```

time: 85.5 us -> 80.2 us (0.938)
  blocking collectives: 46.1 us -> 60.4 us
  Pallas kernels: 15 us -> 5.95 us
  starting transfers between devices: 12.1 us -> 3.94 us
  waiting for transfers between devices: 8.11 us -> 0.01 us
  local copies, waits for them, and re-layouts: 1.97 us -> 8.16 us
    all_to_all x2 -> x3, blocking collectives: 46.1 us -> 60.4 us  [exchange(): lax.all_to_all(blocks, axis, split_axis=0, concat_axis=0, tiled=True, axi...]
    pallas_call x5, Pallas kernels: 15 us -> 5.95 us  [call(): pl.pallas_call(kernel, out_shape=[jax.ShapeDtypeStruct(shape, dtype) for...]
    all_to_all x1 -> x0, starting transfers between devices: 8.15 us -> none  [exchange(): lax.all_to_all(blocks, axis, split_axis=0, concat_axis=0, tiled=True, axi...]
    all_to_all x1 -> x0, waiting for transfers between devices: 8.11 us -> none  [exchange(): lax.all_to_all(blocks, axis, split_axis=0, concat_axis=0, tiled=True, axi...]
    unnamed x6 -> x34, local copies, waits for them, and re-layouts: 1.36 us -> 8.16 us
  transfers between devices with their start and end apart: 2 -> 1, of which waited for: 1 -> 0; matrix products, arithmetic and copies ran while one was open for 1% -> 0% of each run, Pallas kernels for 3% -> 2%
where the time goes in v2:
time: 80.2 us; the launch traced here: 79.7 us
  blocking collectives  60.4 us (75%)
  local copies, waits for them, and re-layouts  8.16 us (10%)
  Pallas kernels  5.95 us (7%)
  starting transfers between devices  3.94 us (5%)
  other arithmetic  1.05 us (1%)
    all_to_all x3, blocking collectives, exchange(): lax.all_to_all(blocks, axis, split_axis=0, concat_axis=0, tiled=True, axi...  60.4 us
    unnamed x34, local copies, waits for them, and re-layouts  8.16 us
    pallas_call x5, Pallas kernels, call(): pl.pallas_call(kernel, out_shape=[jax.ShapeDtypeStruct(shape, dtype) for...  5.95 us
    ppermute x1, starting transfers between devices, from_behind(): lax.ppermute(value, axis, [(source, source + 1) for source in range(count...  3.94 us
  transfers between devices with their start and end apart: 1, of which 0 were waited for; matrix products, arithmetic and copies ran while one was open for 0% of the time, Pallas kernels for 2%

profile of v2, /device:TPU:1, one launch (start us, length us, event | category | flops | bytes accessed | tf_op | source)
XLA Modules:
  0.0 79.7 jit_solution(11477000302151779146)
XLA Ops:
  0.0 1.1 %multiply_convert_fusion = bf16[128,512]{1,0:T(8,128)(2,1)S(1)} fusion(bf16[256,512]{1,0:T(8,128)(2,1)} %value.1, bf16[256,512]{1,0:T(8,128)(2,1)} %first.1), kind=kLoop, calls=%fused_computation | loop fusion | flops 262144 | bytes 393216 | tf_op jit(solution)/shard_map/convert_element_type | solution.py:271
  1.1 0.0 copy-start.15
  1.1 3.9 %collective-permute-start = (bf16[128,512]{1,0:T(8,128)(2,1)S(1)}, bf16[128,512]{1,0:T(8,128)(2,1)S(1)}, u32[]{:S(2)}, u32[]{:S(2)}) collective-permute-start(bf16[128,512]{1,0:T(8,128)(2,1)S(1)} %multiply_convert_fusion), channel_id=1, source_target_pairs={{0,16},{16,32},{32,48},{48,64},{64,80},{80,96},{96,112},{112,128},... | collective-permute-start | bytes 393224 | tf_op jit(solution)/shard_map/ppermute | solution.py:48
  5.1 0.0 copy-start.1
  5.1 0.9 %copy-done.1 = bf16[256,384]{1,0:T(8,128)(2,1)S(1)} copy-done((bf16[256,384]{1,0:T(8,128)(2,1)S(1)}, bf16[256,384]{1,0:T(8,128)(2,1)}, u32[]{:S(2)}) %copy-start.1) | copy-done | bytes 196632
  6.0 0.9 %copy-done.3 = bf16[256,384]{1,0:T(8,128)(2,1)S(1)} copy-done((bf16[256,384]{1,0:T(8,128)(2,1)S(1)}, bf16[256,384]{1,0:T(8,128)(2,1)}, u32[]{:S(2)}) %copy-start.3) | copy-done | bytes 196632
  6.9 0.9 %copy-done.5 = bf16[256,512]{1,0:T(8,128)(2,1)S(1)} copy-done((bf16[256,512]{1,0:T(8,128)(2,1)S(1)}, bf16[256,512]{1,0:T(8,128)(2,1)}, u32[]{:S(2)}) %copy-start.5) | copy-done | bytes 262168
  7.9 0.9 %copy-done.6 = bf16[256,512]{1,0:T(8,128)(2,1)S(1)} copy-done((bf16[256,512]{1,0:T(8,128)(2,1)S(1)}, bf16[256,512]{1,0:T(8,128)(2,1)}, u32[]{:S(2)}) %copy-start.6) | copy-done | bytes 262168
  8.8 0.9 %copy-done.9 = bf16[384,128]{1,0:T(8,128)(2,1)S(1)} copy-done((bf16[384,128]{1,0:T(8,128)(2,1)S(1)}, bf16[384,128]{1,0:T(8,128)(2,1)}, u32[]{:S(2)}) %copy-start.9) | copy-done | bytes 98328
  9.7 0.9 %copy-done.11 = f32[128,512]{1,0:T(8,128)S(1)} copy-done((f32[128,512]{1,0:T(8,128)S(1)}, f32[128,512]{1,0:T(8,128)}, u32[]{:S(2)}) %copy-start.11) | copy-done | bytes 262168
  10.7 0.9 %copy-done.12 = bf16[384,256]{1,0:T(8,128)(2,1)S(1)} copy-done((bf16[384,256]{1,0:T(8,128)(2,1)S(1)}, bf16[384,256]{1,0:T(8,128)(2,1)}, u32[]{:S(2)}) %copy-start.12) | copy-done | bytes 196632
  11.6 0.9 %copy-done.13 = bf16[384,256]{1,0:T(8,128)(2,1)S(1)} copy-done((bf16[384,256]{1,0:T(8,128)(2,1)S(1)}, bf16[384,256]{1,0:T(8,128)(2,1)}, u32[]{:S(2)}) %copy-start.13) | copy-done | bytes 196632
  12.5 0.7 copy-done.16
  13.2 1.8 %shard_map.145 = (f32[384,512]{1,0:T(8,128)S(1)}, f32[128,512]{1,0:T(8,128)S(1)}, bf16[128,512]{1,0:T(8,128)(2,1)S(1)}, f32[512,128]{1,0:T(8,128)S(1)}, f32[64,128]{1,0:T(8,128)S(1)}, /*index=5*/f32[2,512]{1,0:T(2,128)S(1)}) custom-call(bf16[256,512]{1,0:T(8,128)(2,1)S(1)} %copy-done.5, bf16[256,512]{1,0:T(8,128)(2,1)S(1)} %copy-done.6, ...), custom_call_target="tpu_custom_call" | custom-call | tf_op jit(solution)/shard_map/pallas_call | solution.py:241
  15.0 0.0 collective-permute-done.halo
  15.1 0.0 copy-done.2
  15.1 1.4 %shard_map.146 = (bf16[128,512]{1,0:T(8,128)(2,1)S(1)}, f32[512,128]{1,0:T(8,128)S(1)}, f32[64,128]{1,0:T(8,128)S(1)}, f32[512,128]{1,0:T(8,128)S(1)}) custom-call(f32[384,512]{1,0:T(8,128)S(1)} %get-tuple-element.19.response, f32[128,512]{1,0:T(8,128)S(1)} %get-tuple-element.20.short, bf16[128,512]{1,0:T(8,128)(2,1)S(1)} %collective-permute-done.halo, ...), custom_call_target="tpu_custom_call" | custom-call | tf_op jit(solution)/shard_map/pallas_call | solution.py:241
  16.4 14.7 %all_to_all.15 = f32[8,64,128]{2,1,0:T(8,128)S(1)} all-to-all(f32[8,64,128]{2,1,0:T(8,128)S(1)} %bitcast.10), channel_id=1, replica_groups={{0,16,32,48,64,80,96,112},{128,144,160,176,192,208,224,240},{256,272,28..., dimensions={0} | all-to-all | bytes 524288 | tf_op jit(solution)/shard_map/all_to_all | solution.py:54
  31.2 0.0 copy-start.10
  31.2 0.0 copy-start.14
  31.2 26.6 %all_to_all.16 = f32[8,64,128]{2,1,0:T(8,128)S(1)} all-to-all(f32[8,64,128]{2,1,0:T(8,128)S(1)} %bitcast.11), channel_id=1, replica_groups={{0,128,256,384,512,640,768,896},{16,144,272,400,528,656,784,912},{32,16..., dimensions={0} | all-to-all | bytes 524288 | tf_op jit(solution)/shard_map/all_to_all | solution.py:54
  57.8 1.9 %shard_map.148 = (f32[256,512]{1,0:T(8,128)S(1)}, f32[128,128]{1,0:T(8,128)S(1)}) custom-call(bf16[128,512]{1,0:T(8,128)(2,1)S(1)} %get-tuple-element.22.mixed_head, bf16[128,512]{1,0:T(8,128)(2,1)S(1)} %get-tuple-element.23.mixed_tail, f32[512,128]{1,0:T(8,128)S(1)} %get-tuple-element.24.prefix_head, f32[512,128]{1,0:T(8,128)S(1)} %get-tuple-element.25.prefix_tail, ...), custom_call_target="tpu_custom_call" | custom-call | tf_op jit(solution)/shard_map/pallas_call | solution.py:241
  59.7 19.1 %all_to_all.17 = f32[16,8,128]{2,1,0:T(8,128)S(1)} all-to-all(f32[16,8,128]{2,1,0:T(8,128)S(1)} %bitcast.13), channel_id=1, replica_groups=mesh['context'=64,'channel'=16] {'channel'}, dimensions={0} | all-to-all | bytes 131072 | tf_op jit(solution)/shard_map/all_to_all | solution.py:54
  78.8 0.8 %shard_map.149 = bf16[256,512]{1,0:T(8,128)(2,1)} custom-call(f32[128,128]{1,0:T(8,128)S(1)} %bitcast.12, f32[256,512]{1,0:T(8,128)S(1)} %get-tuple-element.32.gated), custom_call_target="tpu_custom_call" | custom-call | tf_op jit(solution)/shard_map/pallas_call | solution.py:241
  (21 shorter events, 0.1 us)
Async XLA Ops:
  0.0 5.0 %copy-start.8 = (bf16[384,128]{1,0:T(8,128)(2,1)S(1)}, bf16[384,128]{1,0:T(8,128)(2,1)}, u32[]{:S(2)}) copy-start(bf16[384,128]{1,0:T(8,128)(2,1)} %constant.13.clone.head_lo) | copy-start | bytes 294916
  0.0 5.0 %copy-start.7 = (f32[16,512]{1,0:T(8,128)S(1)}, f32[16,512]{1,0:T(8,128)}, u32[]{:S(2)}) copy-start(f32[16,512]{1,0:T(8,128)} %rate.7) | copy-start | bytes 98308
  0.0 5.0 %copy-start = (bf16[256,512]{1,0:T(8,128)(2,1)S(1)}, bf16[256,512]{1,0:T(8,128)(2,1)}, u32[]{:S(2)}) copy-start(bf16[256,512]{1,0:T(8,128)(2,1)} %gate.4) | copy-start | bytes 786436
  1.1 4.0 %copy-start.15 = (f32[512]{0:T(512)S(1)}, f32[512]{0:T(512)}, u32[]{:S(2)}) copy-start(f32[512]{0:T(512)} %param.22) | copy-start | bytes 6148
  1.1 14.0 %collective-permute-start = (bf16[128,512]{1,0:T(8,128)(2,1)S(1)}, bf16[128,512]{1,0:T(8,128)(2,1)S(1)}, u32[]{:S(2)}, u32[]{:S(2)}) collective-permute-start(bf16[128,512]{1,0:T(8,128)(2,1)S(1)} %multiply_convert_fusion), channel_id=1, source_target_pairs={{0,16},{16,32},{32,48},{48,64},{64,80},{80,96},{96,112},{112,128},... | collective-permute-start | bytes 393224 | tf_op jit(solution)/shard_map/ppermute | solution.py:48
  5.1 0.9 %copy-start.1 = (bf16[256,384]{1,0:T(8,128)(2,1)S(1)}, bf16[256,384]{1,0:T(8,128)(2,1)}, u32[]{:S(2)}) copy-start(bf16[256,384]{1,0:T(8,128)(2,1)} %constant.17.clone.back_lo) | copy-start | bytes 589828
  6.0 0.9 %copy-start.3 = (bf16[256,384]{1,0:T(8,128)(2,1)S(1)}, bf16[256,384]{1,0:T(8,128)(2,1)}, u32[]{:S(2)}) copy-start(bf16[256,384]{1,0:T(8,128)(2,1)} %constant.16.clone.back_hi) | copy-start | bytes 589828
  6.9 0.9 %copy-start.5 = (bf16[256,512]{1,0:T(8,128)(2,1)S(1)}, bf16[256,512]{1,0:T(8,128)(2,1)}, u32[]{:S(2)}) copy-start(bf16[256,512]{1,0:T(8,128)(2,1)} %first.1) | copy-start | bytes 786436
  7.9 0.9 %copy-start.6 = (bf16[256,512]{1,0:T(8,128)(2,1)S(1)}, bf16[256,512]{1,0:T(8,128)(2,1)}, u32[]{:S(2)}) copy-start(bf16[256,512]{1,0:T(8,128)(2,1)} %value.1) | copy-start | bytes 786436
  8.8 0.9 %copy-start.9 = (bf16[384,128]{1,0:T(8,128)(2,1)S(1)}, bf16[384,128]{1,0:T(8,128)(2,1)}, u32[]{:S(2)}) copy-start(bf16[384,128]{1,0:T(8,128)(2,1)} %constant.12.clone.head_hi) | copy-start | bytes 294916
  9.7 0.9 %copy-start.11 = (f32[128,512]{1,0:T(8,128)S(1)}, f32[128,512]{1,0:T(8,128)}, u32[]{:S(2)}) copy-start(f32[128,512]{1,0:T(8,128)} %taps.1) | copy-start | bytes 786436
  10.7 0.9 %copy-start.12 = (bf16[384,256]{1,0:T(8,128)(2,1)S(1)}, bf16[384,256]{1,0:T(8,128)(2,1)}, u32[]{:S(2)}) copy-start(bf16[384,256]{1,0:T(8,128)(2,1)} %constant.15.clone.body_lo) | copy-start | bytes 589828
  11.6 0.9 %copy-start.13 = (bf16[384,256]{1,0:T(8,128)(2,1)S(1)}, bf16[384,256]{1,0:T(8,128)(2,1)}, u32[]{:S(2)}) copy-start(bf16[384,256]{1,0:T(8,128)(2,1)} %constant.14.clone.body_hi) | copy-start | bytes 589828
  12.5 0.7 copy-start.16
  13.2 1.8 %copy-start.2 = (bf16[256,384]{1,0:T(8,128)(2,1)S(1)}, bf16[256,384]{1,0:T(8,128)(2,1)}, u32[]{:S(2)}) copy-start(bf16[256,384]{1,0:T(8,128)(2,1)} %constant.17.clone.back_lo) | copy-start | bytes 589828
  13.2 1.9 %copy-start.4 = (bf16[256,384]{1,0:T(8,128)(2,1)S(1)}, bf16[256,384]{1,0:T(8,128)(2,1)}, u32[]{:S(2)}) copy-start(bf16[256,384]{1,0:T(8,128)(2,1)} %constant.16.clone.back_hi) | copy-start | bytes 589828
  31.2 26.6 %copy-start.10 = (bf16[256,512]{1,0:T(8,128)(2,1)S(1)}, bf16[256,512]{1,0:T(8,128)(2,1)}, u32[]{:S(2)}) copy-start(bf16[256,512]{1,0:T(8,128)(2,1)} %gate.5) | copy-start | bytes 786436
  31.2 26.6 %copy-start.14 = (f32[16,512]{1,0:T(8,128)S(1)}, f32[16,512]{1,0:T(8,128)}, u32[]{:S(2)}) copy-start(f32[16,512]{1,0:T(8,128)} %residue.1) | copy-start | bytes 98308

commit v3 on v2

--- a/solution.py
+++ b/solution.py
@@ -97,22 +97,44 @@
 
 
 def local_kernel(
-    first, value, taps, gate, head_hi, head_lo, body_hi, body_lo, back_hi, back_lo, rate, skip, gain,
-    response_ref, short_ref, mixed_ref, prefix_ref, end_ref, rows_ref, steps_ref,
+    first, value, taps, gate, out_gate, rate, residue, skip, gain,
+    head_hi, head_lo, body_hi, body_lo, back_hi, back_lo,
+    response_ref, short_ref, mixed_ref, prefix_ref, end_ref,
+    gate_ref, out_gate_ref, rate_ref, residue_ref, skip_ref, gain_ref,
+    head_hi_ref, head_lo_ref, back_hi_ref, back_lo_ref,
+    first_ref, value_ref, taps_ref, body_hi_ref, body_lo_ref, steps_ref, sems,
 ):
-    rows_ref[0:1] = skip[...]
-    rows_ref[1:2] = gain[...]
-    product = (first[...].astype(jnp.float32) * value[...].astype(jnp.float32)).astype(jnp.bfloat16)
-    spectrum = dot(body_hi[...], product) + dot(body_lo[...], product)
-    tap_hi, tap_lo = split(taps[...])
-    response = dot(head_hi[...], tap_hi) + dot(head_hi[...], tap_lo) + dot(head_lo[...], tap_hi)
+    moves = (
+        (first, first_ref), (value, value_ref), (body_hi, body_hi_ref), (body_lo, body_lo_ref),
+        (taps, taps_ref), (head_hi, head_hi_ref), (head_lo, head_lo_ref), (back_hi, back_hi_ref),
+        (back_lo, back_lo_ref), (gate, gate_ref), (rate, rate_ref), (residue, residue_ref),
+        (skip, skip_ref), (gain, gain_ref), (out_gate, out_gate_ref),
+    )
+    copies = [
+        pltpu.make_async_copy(source, target, sems.at[index])
+        for index, (source, target) in enumerate(moves)
+    ]
+    for copy in copies:
+        copy.start()
+    for copy in copies[:4]:
+        copy.wait()
+    product = (first_ref[...].astype(jnp.float32) * value_ref[...].astype(jnp.float32)).astype(
+        jnp.bfloat16
+    )
+    spectrum = dot(body_hi_ref[...], product) + dot(body_lo_ref[...], product)
+    for copy in copies[4:]:
+        copy.wait()
+    tap_hi, tap_lo = split(taps_ref[...])
+    response = (
+        dot(head_hi_ref[...], tap_hi) + dot(head_hi_ref[...], tap_lo) + dot(head_lo_ref[...], tap_hi)
+    )
     response_ref[...] = response
-    short = respond(spectrum, response, back_hi[...], back_lo[...])
+    short = respond(spectrum, response, back_hi_ref[...], back_lo_ref[...])
     half = mixed_ref.shape[0]
     short_ref[...] = short[:half]
-    mixed = (gate[half:].astype(jnp.float32) * short[half:]).astype(jnp.bfloat16)
+    mixed = (gate_ref[half:].astype(jnp.float32) * short[half:]).astype(jnp.bfloat16)
     mixed_ref[...] = mixed
-    end_states(mixed, rate, prefix_ref, end_ref, steps_ref)
+    end_states(mixed, rate_ref, prefix_ref, end_ref, steps_ref)
 
 
 def halo_kernel(
@@ -159,7 +181,7 @@
 
 
 def long_kernel(
-    mixed_head, mixed_tail, prefix_head, prefix_tail, end, totals, ahead, rate, residue, per_channel, gate,
+    mixed_head, mixed_tail, prefix_head, prefix_tail, end, totals, ahead, rate, residue, skip, gain, gate,
     gated_ref, power_ref, steps_ref, long_ref, *, side,
 ):
     half, width = mixed_head.shape
@@ -202,11 +224,11 @@
                     sums = [a + b for a, b in zip(sums[::2], sums[1::2])]
                 long_ref[pl.ds(base + step, SUB, stride=strip)] = sums[0]
             out = (
-                long_ref[base : base + half] + per_channel[0:1, lanes] * steps_ref[base : base + half]
+                long_ref[base : base + half] + skip[:, lanes] * steps_ref[base : base + half]
             ).astype(jnp.bfloat16)
             tokens = slice(part * half, (part + 1) * half)
             gated = gate[tokens, lanes].astype(jnp.float32) * out.astype(jnp.float32)
-            gated_ref[tokens, lanes] = gated * per_channel[1:2, lanes]
+            gated_ref[tokens, lanes] = gated * gain[:, lanes]
             squares[part] = squares[part] + gated * gated
     packed = jnp.zeros((SUB, LANES), jnp.float32)
     for part in range(2):
@@ -236,14 +258,17 @@
             out_ref[tokens, lanes] = (gated[tokens, lanes] * column).astype(jnp.bfloat16)
 
 
-def call(kernel, outs, *args, scratch=()):
+def call(kernel, outs, *args, scratch=(), fetch=False):
     vmem = pl.BlockSpec(memory_space=pltpu.VMEM)
+    if fetch and not INTERPRET:
+        args = [pltpu.with_memory_space_constraint(array, pltpu.HBM) for array in args]
+    scratches = [pltpu.VMEM(shape, dtype) for shape, dtype in scratch]
     return pl.pallas_call(
         kernel,
         out_shape=[jax.ShapeDtypeStruct(shape, dtype) for shape, dtype in outs],
-        in_specs=[vmem] * len(args),
+        in_specs=[pl.BlockSpec(memory_space=pltpu.HBM) if fetch else vmem] * len(args),
         out_specs=[vmem] * len(outs),
-        scratch_shapes=[pltpu.VMEM(shape, jnp.float32) for shape in scratch],
+        scratch_shapes=scratches + ([pltpu.SemaphoreType.DMA((len(args),))] if fetch else []),
         compiler_params=pltpu.CompilerParams(vmem_limit_bytes=16 << 20),
         interpret=INTERPRET,
     )(*args)
@@ -275,15 +300,25 @@
     assert half == taps == LANES
     lots = modes * tiles
     strips = (lots * SUB, LANES)
-    response, short, mixed_tail, prefix_tail, last, per_channel = call(
+    skip, gain = li_skip[None], norm_gain[None]
+    kept = [short_gate, out_gate, li_rate, li_residue, skip, gain]
+    kept += [head_hi, head_lo, back_hi, back_lo]
+    (
+        response, short, mixed_tail, prefix_tail, last,
+        gate, last_gate, rate, residue, skip, gain, head_hi, head_lo, back_hi, back_lo,
+    ) = call(
         local_kernel,
         [
             ((rows + taps, width), f32), ((half, width), f32), ((half, width), bf16),
-            (strips, f32), ((lots, LANES), f32), ((2, width), f32),
-        ],
-        first_stream, value_stream, mr_filter, short_gate,
-        head_hi, head_lo, body_hi, body_lo, back_hi, back_lo, li_rate, li_skip[None], norm_gain[None],
-        scratch=[(tiles * half, LANES)],
+            (strips, f32), ((lots, LANES), f32),
+        ] + [(array.shape, array.dtype) for array in kept],
+        first_stream, value_stream, mr_filter, short_gate, out_gate, li_rate, li_residue, skip, gain,
+        head_hi, head_lo, body_hi, body_lo, back_hi, back_lo,
+        scratch=[
+            (array.shape, array.dtype)
+            for array in (first_stream, value_stream, mr_filter, body_hi, body_lo)
+        ] + [((tiles * half, LANES), f32)],
+        fetch=True,
     )
     side = math.isqrt(lax.axis_size("context"))
     along_x = [[z * side + x for x in range(side)] for z in range(side)]
@@ -294,14 +329,14 @@
             ((half, width), bf16), (strips, f32), ((lots, LANES), f32),
             ((side * lots, LANES), f32),
         ],
-        response, short, before, short_gate, head_hi, head_lo, back_hi, back_lo, li_rate, last,
-        scratch=[(tiles * half, LANES)],
+        response, short, before, gate, head_hi, head_lo, back_hi, back_lo, rate, last,
+        scratch=[((tiles * half, LANES), f32)],
     )
     states = exchange(states, "context", side, along_x)
     ahead, totals = call(
         functools.partial(row_kernel, rows=rows, side=side),
         [((lots, LANES), f32), ((side * lots, LANES), f32)],
-        states, li_rate,
+        states, rate,
     )
     totals = exchange(totals, "context", side, along_z)
     peers = lax.axis_size("channel")
@@ -309,8 +344,8 @@
         functools.partial(long_kernel, side=side),
         [((rows, width), f32), ((peers * SUB, LANES), f32)],
         mixed_head, mixed_tail, prefix_head, prefix_tail, end, totals, ahead,
-        li_rate, li_residue, per_channel, out_gate,
-        scratch=[(tiles * rows, LANES), (tiles * rows, LANES)],
+        rate, residue, skip, gain, last_gate,
+        scratch=[((tiles * rows, LANES), f32), ((tiles * rows, LANES), f32)],
     )
     powers = exchange(power, "channel", peers, None)
     return call(

time: 80.2 us -> 74.9 us (0.934)
  local copies, waits for them, and re-layouts: 8.16 us -> 0 us
  blocking collectives: 60.4 us -> 62.2 us
  Pallas kernels: 5.95 us -> 7.46 us
    unnamed x34 -> x0, local copies, waits for them, and re-layouts: 8.16 us -> none
    all_to_all x3, blocking collectives: 60.4 us -> 62.2 us  [exchange(): lax.all_to_all(blocks, axis, split_axis=0, concat_axis=0, tiled=True, axi...]
    pallas_call x5, Pallas kernels: 5.95 us -> 7.46 us  [call(): pl.pallas_call(kernel, out_shape=[jax.ShapeDtypeStruct(shape, dtype) for...]
  transfers between devices with their start and end apart: 1 -> 1, of which waited for: 0 -> 0; matrix products, arithmetic and copies ran while one was open for 0% -> 0% of each run, Pallas kernels for 2% -> 5%
where the time goes in v3:
time: 74.9 us; the launch traced here: 74.6 us
  blocking collectives  62.2 us (83%)
  Pallas kernels  7.46 us (10%)
  starting transfers between devices  3.94 us (5%)
  other arithmetic  1 us (1%)
    all_to_all x3, blocking collectives, exchange(): lax.all_to_all(blocks, axis, split_axis=0, concat_axis=0, tiled=True, axi...  62.2 us
    pallas_call x5, Pallas kernels, call(): pl.pallas_call(kernel, out_shape=[jax.ShapeDtypeStruct(shape, dtype) for...  7.46 us
    ppermute x1, starting transfers between devices, from_behind(): lax.ppermute(value, axis, [(source, source + 1) for source in range(count...  3.94 us
  transfers between devices with their start and end apart: 1, of which 0 were waited for; matrix products, arithmetic and copies ran while one was open for 0% of the time, Pallas kernels for 5%

profile of v3, /device:TPU:1, one launch (start us, length us, event | category | flops | bytes accessed | tf_op | source)
XLA Modules:
  0.0 74.6 jit_solution(576079310274565047)
XLA Ops:
  0.0 1.0 %multiply_convert_fusion = bf16[128,512]{1,0:T(8,128)(2,1)S(1)} fusion(bf16[256,512]{1,0:T(8,128)(2,1)} %value.1, bf16[256,512]{1,0:T(8,128)(2,1)} %first.1), kind=kLoop, calls=%fused_computation | loop fusion | flops 262144 | bytes 393216 | tf_op jit(solution)/shard_map/convert_element_type | solution.py:296
  1.0 3.9 %collective-permute-start = (bf16[128,512]{1,0:T(8,128)(2,1)S(1)}, bf16[128,512]{1,0:T(8,128)(2,1)S(1)}, u32[]{:S(2)}, u32[]{:S(2)}) collective-permute-start(bf16[128,512]{1,0:T(8,128)(2,1)S(1)} %multiply_convert_fusion), channel_id=1, source_target_pairs={{0,16},{16,32},{32,48},{48,64},{64,80},{80,96},{96,112},{112,128},... | collective-permute-start | bytes 393224 | tf_op jit(solution)/shard_map/ppermute | solution.py:48
  5.0 3.4 %shard_map.145 = (f32[384,512]{1,0:T(8,128)S(1)}, f32[128,512]{1,0:T(8,128)S(1)}, bf16[128,512]{1,0:T(8,128)(2,1)S(1)}, f32[512,128]{1,0:T(8,128)S(1)}, f32[64,1...) custom-call(bf16[256,512]{1,0:T(8,128)(2,1)} %first.1, ...), custom_call_target="tpu_custom_call" | custom-call | tf_op jit(solution)/shard_map/pallas_call | solution.py:266
  8.3 0.0 collective-permute-done.halo
  8.3 1.3 %shard_map.146 = (bf16[128,512]{1,0:T(8,128)(2,1)S(1)}, f32[512,128]{1,0:T(8,128)S(1)}, f32[64,128]{1,0:T(8,128)S(1)}, f32[512,128]{1,0:T(8,128)S(1)}) custom-call(f32[384,512]{1,0:T(8,128)S(1)} %get-tuple-element.28.response, f32[128,512]{1,0:T(8,128)S(1)} %get-tuple-element.29.short, bf16[128,512]{1,0:T(8,128)(2,1)S(1)} %collective-permute-done.halo, ...), custom_call_target="tpu_custom_call" | custom-call | tf_op jit(solution)/shard_map/pallas_call | solution.py:266
  9.7 16.7 %all_to_all.15 = f32[8,64,128]{2,1,0:T(8,128)S(1)} all-to-all(f32[8,64,128]{2,1,0:T(8,128)S(1)} %bitcast.10), channel_id=1, replica_groups={{0,16,32,48,64,80,96,112},{128,144,160,176,192,208,224,240},{256,272,28..., dimensions={0} | all-to-all | bytes 524288 | tf_op jit(solution)/shard_map/all_to_all | solution.py:54
  26.4 25.8 %all_to_all.16 = f32[8,64,128]{2,1,0:T(8,128)S(1)} all-to-all(f32[8,64,128]{2,1,0:T(8,128)S(1)} %bitcast.11), channel_id=1, replica_groups={{0,128,256,384,512,640,768,896},{16,144,272,400,528,656,784,912},{32,16..., dimensions={0} | all-to-all | bytes 524288 | tf_op jit(solution)/shard_map/all_to_all | solution.py:54
  52.2 1.9 %shard_map.148 = (f32[256,512]{1,0:T(8,128)S(1)}, f32[128,128]{1,0:T(8,128)S(1)}) custom-call(bf16[128,512]{1,0:T(8,128)(2,1)S(1)} %get-tuple-element.37.mixed_head, bf16[128,512]{1,0:T(8,128)(2,1)S(1)} %get-tuple-element.38.mixed_tail, f32[512,128]{1,0:T(8,128)S(1)} %get-tuple-element.39.prefix_head, f32[512,128]{1,0:T(8,128)S(1)} %get-tuple-element.40.prefix_tail, ...), custom_call_target="tpu_custom_call" | custom-call | tf_op jit(solution)/shard_map/pallas_call | solution.py:266
  54.1 19.7 %all_to_all.17 = f32[16,8,128]{2,1,0:T(8,128)S(1)} all-to-all(f32[16,8,128]{2,1,0:T(8,128)S(1)} %bitcast.13), channel_id=1, replica_groups=mesh['context'=64,'channel'=16] {'channel'}, dimensions={0} | all-to-all | bytes 131072 | tf_op jit(solution)/shard_map/all_to_all | solution.py:54
  73.8 0.8 %shard_map.149 = bf16[256,512]{1,0:T(8,128)(2,1)} custom-call(f32[128,128]{1,0:T(8,128)S(1)} %bitcast.12, f32[256,512]{1,0:T(8,128)S(1)} %get-tuple-element.50.gated), custom_call_target="tpu_custom_call" | custom-call | tf_op jit(solution)/shard_map/pallas_call | solution.py:266
  (1 shorter events, 0.0 us)
Async XLA Ops:
  1.0 7.3 %collective-permute-start = (bf16[128,512]{1,0:T(8,128)(2,1)S(1)}, bf16[128,512]{1,0:T(8,128)(2,1)S(1)}, u32[]{:S(2)}, u32[]{:S(2)}) collective-permute-start(bf16[128,512]{1,0:T(8,128)(2,1)S(1)} %multiply_convert_fusion), channel_id=1, source_target_pairs={{0,16},{16,32},{32,48},{48,64},{64,80},{80,96},{96,112},{112,128},... | collective-permute-start | bytes 393224 | tf_op jit(solution)/shard_map/ppermute | solution.py:48
